TPU v7x, 32 devices: a whole 2x2x4 slice. The times are simulated.
32 devices in a mesh: tm: 2 (over x), vox: 8 (over z, y), feat: 2 (over core).
Axes of the slice: x: 2, y: 2, z: 4, core: 2. Of those that a mesh axis runs over, the one named last changes fastest.
Arguments:
- design_matrix: bfloat16 [256, 4096], P(None, ('tm', 'feat')), may hold values from -6 to 6
- measured_signals: bfloat16 [256, 16384], P('tm', 'vox'), may hold values from -6 to 6
- predictor_group_label: int32 [4096], P('vox'), may hold values from 0 to 3
- shrinkage_weights: float32 [2, 4], replicated, may hold values from 0.1 to 10
- target_shrink_choice: int32 [256], P('vox'), may hold values from 0 to 1
Outputs:
- trailing: float32 [2, 4096, 4096], P(None, ('tm', 'feat'), 'vox')
- right_sides: float32 [4096, 16384], P(('tm', 'feat'), 'vox')
All inputs are finite; a program needn't handle non-finite values.
Results may differ from a plain program's by a relative error of at most 0.0003.
Values may be sent and summed in bfloat16 or wider, within the bound.
No kernel may reach another device: no remote copies, remote signals or barrier semaphores. Data moves between devices by JAX's collectives and lax.ppermute only.
A program may use at most 128 MiB of HBM per device.

v0:
```python
import math
import jax
import jax.numpy as jnp
from jax import lax
from jax.sharding import PartitionSpec as P

P_SIZE = 4096
PREDICTOR_GROUPS = 4
SHRINK_OPTIONS = 2
GROUP = 64


def spread(block, axis, owner):
    block = jnp.where(lax.axis_index(axis) == owner, block, jnp.zeros_like(block))
    return lax.psum(block, axis)


def local(
    design_matrix, measured_signals, predictor_group_label, shrinkage_weights, target_shrink_choice
):
    row_index = lax.axis_index(("tm", "feat"))
    column_index = lax.axis_index("vox")
    total_time, row_block = design_matrix.shape
    column_width = P_SIZE // lax.axis_size("vox")
    voxel_count = measured_signals.shape[1]
    source_row = column_index * column_width // row_block
    own_columns = lax.dynamic_slice_in_dim(
        design_matrix, column_index * column_width - source_row * row_block, column_width, 1
    )
    shared_columns = spread(own_columns, ("tm", "feat"), source_row)
    gram_tile = (
        jnp.einsum("tr,tc->rc", design_matrix, shared_columns, preferred_element_type=jnp.float32)
        / total_time
    )
    global_rows = row_index * row_block + jnp.arange(row_block)
    global_columns = column_index * column_width + jnp.arange(column_width)
    group_membership_mask = (
        predictor_group_label[:, None] == jnp.arange(PREDICTOR_GROUPS)[None, :]
    ).astype(jnp.float32)
    predictor_shrinkage = jnp.dot(
        shrinkage_weights, group_membership_mask.T, precision=lax.Precision.HIGHEST
    )
    on_diagonal = (global_rows[:, None] == global_columns[None, :])[None, :, :]
    system_tiles = gram_tile[None, :, :] + jnp.where(
        on_diagonal, predictor_shrinkage[:, None, :], 0.0
    )
    right_sides = jnp.einsum(
        "tr,tv->rv",
        design_matrix,
        lax.all_gather(measured_signals, "tm", axis=0, tiled=True),
        preferred_element_type=jnp.float32,
    )
    right_sides = right_sides / math.sqrt(total_time)
    first_ridge = jnp.repeat(target_shrink_choice, GROUP) == 0
    identity_block = jnp.broadcast_to(
        jnp.eye(column_width, dtype=jnp.float32), (SHRINK_OPTIONS, column_width, column_width)
    )
    diagonal_owner = 0 // row_block
    local_offset = 0 - diagonal_owner * row_block
    diagonal = system_tiles[:, local_offset : local_offset + column_width, :]
    diagonal = spread(diagonal, ("tm", "feat"), diagonal_owner)
    diagonal = jnp.where(column_index == 0, diagonal, identity_block)
    factor = jnp.linalg.cholesky(diagonal)
    solved = lax.linalg.triangular_solve(
        factor, system_tiles, left_side=False, lower=True, transpose_a=True
    )
    solved = jnp.where((global_rows >= 0)[None, :, None], solved, 0.0)
    panel, factor = (spread(solved, "vox", 0), spread(factor, "vox", 0))
    panel_slice = lax.dynamic_slice_in_dim(
        panel, column_index * column_width - source_row * row_block, column_width, 1
    )
    partner_rows = spread(panel_slice, ("tm", "feat"), source_row)
    block_sides = jnp.broadcast_to(
        right_sides[local_offset : local_offset + column_width],
        (SHRINK_OPTIONS, column_width, voxel_count),
    )
    solutions = lax.linalg.triangular_solve(factor, block_sides, left_side=True, lower=True)
    solved_sides = jnp.where(first_ridge[None, :], solutions[0], solutions[1])
    solved_sides = spread(solved_sides, ("tm", "feat"), diagonal_owner)
    system_tiles = system_tiles - jnp.einsum(
        "brk,bck->brc", panel, partner_rows, precision=lax.Precision.HIGHEST
    )
    update_first = jnp.dot(panel[0], solved_sides, precision=lax.Precision.HIGHEST)
    update_second = jnp.dot(panel[1], solved_sides, precision=lax.Precision.HIGHEST)
    right_sides = right_sides - jnp.where(first_ridge[None, :], update_first, update_second)
    inside_block = (global_rows >= 0) & (global_rows < column_width)
    placed = (
        jnp.zeros((row_block, voxel_count), jnp.float32)
        .at[local_offset : local_offset + column_width]
        .set(solved_sides)
    )
    right_sides = jnp.where(inside_block[:, None], placed, right_sides)
    return (system_tiles, right_sides)


def solution(mesh):
    return jax.shard_map(
        local,
        mesh=mesh,
        in_specs=(P(None, ("tm", "feat")), P("tm", "vox"), P("vox"), P(), P("vox")),
        out_specs=(P(None, ("tm", "feat"), "vox"), P(("tm", "feat"), "vox")),
        check_vma=False,
    )
```

profile of v0, /device:TPU:0, one launch (start us, length us, event | category | flops | bytes accessed | tf_op | source)
XLA Modules:
  0.0 928.3 jit_solution(13369854478591453120)
XLA Ops:
  11.3 35.5 %all-reduce.9.cloned.1.call-done = bf16[256,512]{1,0:T(8,128)(2,1)} async-done(((bf16[256,512]{1,0:T(8,128)(2,1)}), bf16[256,512]{1,0:T(8,128)(2,1)}) %all-reduce.9.cloned.1.call-update) | async-done | bytes 262160 | tf_op jit(solution)/shard_map/psum | solution.py:15
  48.8 2.0 copy-done.5
  54.0 61.2 %all-reduce.11.cloned.1.call-done = f32[2,512,512]{1,2,0:T(8,128)} async-done(((f32[2,512,512]{1,2,0:T(8,128)}), f32[2,512,512]{1,2,0:T(8,128)}) %all-reduce.11.cloned.1.call-update) | async-done | bytes 2097168 | tf_op jit(solution)/shard_map/psum | solution.py:15
  115.3 3.3 broadcast_select_fusion
  118.6 3.1 copy.45
  121.7 2.9 fusion.30
  125.9 23.5 %custom-call.37 = f32[2,128,128]{2,1,0:T(8,128)S(1)} custom-call(f32[2,128,128]{2,1,0:T(8,128)S(1)} %cholesky.271), custom_call_target="Cholesky" | custom-call | tf_op jit(solution)/shard_map/jit(cholesky)/cholesky | solution.py:63
  149.4 19.7 %custom-call.38 = f32[2,1,128,128]{2,3,1,0:T(8,128)S(1)} custom-call(f32[2,1,128,128]{3,2,1,0:T(8,128)S(1)} %select_bitcast_fusion.2), custom_call_target="InvertDiagBlocksLowerTriangular" | custom-call | tf_op jit(solution)/shard_map/jit(cholesky)/cholesky | solution.py:63
  170.6 2.3 convolution_subtract_fusion.3
  174.7 24.3 %custom-call.39 = f32[2,128,128]{2,1,0:T(8,128)S(1)} custom-call(f32[2,128,128]{2,1,0:T(8,128)} %cholesky.275), custom_call_target="Cholesky" | custom-call | tf_op jit(solution)/shard_map/jit(cholesky)/cholesky | solution.py:63
  201.2 21.5 %custom-call.40 = f32[2,1,128,128]{2,3,1,0:T(8,128)} custom-call(f32[2,1,128,128]{3,2,1,0:T(8,128)} %select_bitcast_fusion.1), custom_call_target="InvertDiagBlocksLowerTriangular" | custom-call | tf_op jit(solution)/shard_map/jit(cholesky)/cholesky | solution.py:63
  225.4 2.0 convolution_subtract_fusion.4
  227.4 23.5 %custom-call.41 = f32[2,128,128]{2,1,0:T(8,128)S(1)} custom-call(f32[2,128,128]{2,1,0:T(8,128)S(1)} %cholesky.280), custom_call_target="Cholesky" | custom-call | tf_op jit(solution)/shard_map/jit(cholesky)/cholesky | solution.py:63
  251.7 19.7 %custom-call.42 = f32[2,1,128,128]{2,3,1,0:T(8,128)S(1)} custom-call(f32[2,1,128,128]{3,2,1,0:T(8,128)S(1)} %select_bitcast_fusion), custom_call_target="InvertDiagBlocksLowerTriangular" | custom-call | tf_op jit(solution)/shard_map/jit(cholesky)/cholesky | solution.py:63
  272.4 2.0 convolution_subtract_fusion.5
  274.4 23.5 %custom-call.43 = f32[2,128,128]{2,1,0:T(8,128)S(1)} custom-call(f32[2,128,128]{2,1,0:T(8,128)S(1)} %convolution_subtract_fusion.5), custom_call_target="Cholesky" | custom-call | tf_op jit(solution)/shard_map/jit(cholesky)/cholesky | solution.py:63
  299.0 4.3 fusion.31
  303.4 13.0 %while.3 = (s32[]{:T(128)}, f32[2,512,512]{1,2,0:T(8,128)}, s32[4,2]{0,1:T(2,128)S(1)}, f32[4,2,128,128]{3,2,0,1:T(8,128)S(1)}, s32[]{:T(128)}) while((s32[]{:T(128)}, f32[2,512,512]{1,2,0:T(8,128)}, s32[4,2]{0,1:T(2,128)S(1)}, f32[4,2,128,128]{3,2,0,1:T(8,128)S(1)}, s32[]{:T(128)}) %tuple.56), condition=%wide.while_cond.1, body=%wide.while_body.1.sunk | while | flops 2 | bytes 786541 | solution.py:64
  304.1 2.4 constant_dynamic-slice_fusion.9
  307.3 2.4 constant_dynamic-slice_fusion.9
  310.6 2.4 constant_dynamic-slice_fusion.9
  313.9 2.4 constant_dynamic-slice_fusion.9
  316.4 78.8 %custom-call.44 = f32[2,4,128,128]{2,3,1,0:T(8,128)S(1)} custom-call(f32[2,4,128,128]{3,2,1,0:T(8,128)S(1)} %bitcast.114), custom_call_target="InvertDiagBlocksLowerTriangular" | custom-call | tf_op jit(solution)/shard_map/triangular_solve | solution.py:64
  395.2 2.3 fusion.39
  397.5 2.5 convolution_subtract_fusion.2
  401.1 2.3 fusion.33
  404.6 3.2 fusion.36
  408.9 3.0 fusion.8
  412.9 2.5 convolution_multiply_fusion
  415.5 3.4 copy-done.2
  420.6 199.6 %all-reduce.13.cloned.1.call-done = (f32[2,1024,512]{1,2,0:T(8,128)}, f32[2,512,512]{1,2,0:T(8,128)}) async-done(((f32[2,1024,512]{1,2,0:T(8,128)}, f32[2,512,512]{1,2,0:T(8,128)}), (f32[2,1024,512]{1,2,0:T(8,128)}, f32[2,512,512]{1,2,0:T(8,128)})) %all-reduce.13.cloned.1.call-update) | async-done | bytes 6291472 | tf_op jit(solution)/shard_map/psum | solution.py:15
  620.2 3.3 broadcast_select_fusion.1
  624.3 14.4 %while.4 = (s32[]{:T(128)}, f32[2,512,512]{1,2,0:T(8,128)}, s32[4,2]{0,1:T(2,128)S(1)}, f32[4,2,128,128]{3,2,0,1:T(8,128)}, s32[]{:T(128)}) while((s32[]{:T(128)}, f32[2,512,512]{1,2,0:T(8,128)}, s32[4,2]{0,1:T(2,128)S(1)}, f32[4,2,128,128]{3,2,0,1:T(8,128)}, s32[]{:T(128)}) %tuple.74), condition=%wide.while_cond.2, body=%wide.while_body.2.sunk | while | flops 2 | bytes 787049 | solution.py:77
  624.9 2.3 constant_dynamic-slice_fusion.11
  628.5 2.3 constant_dynamic-slice_fusion.11
  632.2 2.3 constant_dynamic-slice_fusion.11
  635.8 2.2 constant_dynamic-slice_fusion.11
  638.8 80.4 %custom-call.45 = f32[2,4,128,128]{2,3,1,0:T(8,128)} custom-call(f32[2,4,128,128]{3,2,1,0:T(8,128)} %bitcast.113), custom_call_target="InvertDiagBlocksLowerTriangular" | custom-call | tf_op jit(solution)/shard_map/triangular_solve | solution.py:77
  719.2 3.3 fusion.41
  722.5 2.9 convolution_subtract_fusion
  727.5 3.4 fusion.19
  732.8 5.1 fusion.22
  743.8 3.3 fusion.7
  747.1 118.8 %all-reduce.15.cloned.1.call-done = (f32[2,512,512]{1,2,0:T(8,128)}, f32[512,2048]{1,0:T(8,128)}) async-done(((f32[2,512,512]{1,2,0:T(8,128)}, f32[512,2048]{1,0:T(8,128)}), (f32[2,512,512]{1,2,0:T(8,128)}, f32[512,2048]{1,0:T(8,128)})) %all-reduce.15.cloned.1.call-update) | async-done | bytes 6291472 | tf_op jit(solution)/shard_map/psum | solution.py:15
  865.9 18.0 %fusion.25 = f32[1024,2048]{1,0:T(8,128)} fusion(f32[512,2048]{1,0:T(8,128)} %get-tuple-element.73, f32[2,1024,512]{1,2,0:T(8,128)} %get-tuple-element.70), kind=kOutput, calls=%fused_computation.38 | convolution fusion | flops 12884901888 | bytes 14680064 | tf_op jit(solution)/shard_map/dot_general | solution.py:83
  883.9 8.8 convolution_subtract_fusion.1
  892.7 5.4 copy.82
  898.0 22.9 %subtract_select_fusion = f32[1024,2048]{1,0:T(8,128)} fusion(f32[1024,2048]{1,0:T(8,128)} %copy-done.2, f32[1024,2048]{1,0:T(8,128)} %fusion.25, f32[512,2048]{1,0:T(8,128)} %get-tuple-element.73, pred[1024]{0:T(1024)(128)(4,1)S(1)} %compare_and_fusion, pred[2048]{0:T(1024)(128)(4,1)S(1)} %eq.72, f32[2,1024,512]{1,2,0:T(8,128)} %get-tuple-element.70), kind=kOutput, calls=%fused_computation.7 | convolution fusion | flops 12891193344 | bytes 35654656 | tf_op jit(solution)/shard_map/dot_general | solution.py:84
  (144 shorter events, 46.2 us)
Async XLA Ops:
  8.0 2.3 copy-start
  8.0 38.7 %all-reduce.9.cloned.1.call-start = ((), (), s32[]{:S(2)}) async-start(), calls=%async_computation | async-start | bytes 524288 | tf_op jit(solution)/shard_map/psum | solution.py:15
  9.8 105.5 %all-reduce.11.cloned.1.call-start = ((), (), s32[]{:S(2)}) async-start(), calls=%async_computation.1 | async-start | bytes 4194304 | tf_op jit(solution)/shard_map/psum | solution.py:15
  10.3 38.5 %copy-start.9 = (pred[1024,512]{0,1:T(8,128)(4,1)}, pred[1024,512]{0,1:T(8,128)(4,1)S(1)}, u32[]{:S(2)}) copy-start(pred[1024,512]{0,1:T(8,128)(4,1)S(1)} %broadcast_compare_fusion) | copy-start | bytes 1572868
  48.8 2.0 copy-start.5
  52.5 360.2 %all-gather.2.cloned.1.call-start = ((), (), s32[]{:S(2)}) async-start(), calls=%async_computation.2 | async-start | bytes 1572864 | tf_op jit(solution)/shard_map/all_gather | solution.py:50
  53.1 567.1 %all-reduce.13.cloned.1.call-start = ((), (), s32[]{:S(2)}) async-start(), calls=%async_computation.3 | async-start | bytes 12582912 | tf_op jit(solution)/shard_map/psum | solution.py:15
  53.3 96.0 %copy-start.20 = (pred[128,128]{1,0:T(8,128)(4,1)}, pred[128,128]{1,0:T(8,128)(4,1)S(1)}, u32[]{:S(2)}) copy-start(pred[128,128]{1,0:T(8,128)(4,1)S(1)} %iota_compare_fusion.4) | copy-start | bytes 49156
  54.0 245.0 %copy-start.14 = (pred[512,512]{0,1:T(8,128)(4,1)}, pred[512,512]{0,1:T(8,128)(4,1)S(1)}, u32[]{:S(2)}) copy-start(pred[512,512]{0,1:T(8,128)(4,1)S(1)} %iota_compare_fusion.1) | copy-start | bytes 786436
  124.5 1.3 copy-start.8
  173.1 50.5 %copy-start.17 = (f32[2,384,128]{2,1,0:T(8,128)S(1)}, f32[2,384,128]{2,1,0:T(8,128)}, u32[]{:S(2)}) copy-start(f32[2,384,128]{2,1,0:T(8,128)} %convolution_subtract_fusion.3) | copy-start | bytes 1179652
  222.7 0.9 copy-start.19
  222.7 1.0 copy-start.22
  222.9 28.1 %copy-start.21 = (pred[128,128]{1,0:T(8,128)(4,1)S(1)}, pred[128,128]{1,0:T(8,128)(4,1)}, u32[]{:S(2)}) copy-start(pred[128,128]{1,0:T(8,128)(4,1)} %copy-done.20) | copy-start | bytes 49156
  223.6 74.3 %copy-start.23 = (pred[128,128]{1,0:T(8,128)(4,1)S(1)}, pred[128,128]{1,0:T(8,128)(4,1)}, u32[]{:S(2)}) copy-start(pred[128,128]{1,0:T(8,128)(4,1)} %iota_compare_fusion.5) | copy-start | bytes 49156
  224.1 1.3 copy-start.7
  397.5 3.6 copy-start.6
  411.8 0.7 copy-start.24
  411.9 1.1 copy-start.13
  411.9 454.0 %all-reduce.15.cloned.1.call-start = ((), (), s32[]{:S(2)}) async-start(), calls=%async_computation.4 | async-start | bytes 12582912 | tf_op jit(solution)/shard_map/psum | solution.py:15
  415.4 3.4 copy-start.2
  418.8 201.4 %copy-start.15 = (pred[512,512]{0,1:T(8,128)(4,1)S(1)}, pred[512,512]{0,1:T(8,128)(4,1)}, u32[]{:S(2)}) copy-start(pred[512,512]{0,1:T(8,128)(4,1)} %copy-done.14) | copy-start | bytes 786436
  719.2 3.3 copy-start.11
  722.5 3.0 copy-start.18
  725.5 2.0 copy-start.12
  739.9 2.2 copy-start.3
  865.9 18.0 %copy-start.4 = (f32[2,1024,512]{1,2,0:T(8,128)S(1)}, f32[2,1024,512]{1,2,0:T(8,128)}, u32[]{:S(2)}) copy-start(f32[2,1024,512]{1,2,0:T(8,128)} %get-tuple-element.70) | copy-start | bytes 12582916
  865.9 18.0 %copy-start.10 = (pred[1024,512]{0,1:T(8,128)(4,1)S(1)}, pred[1024,512]{0,1:T(8,128)(4,1)}, u32[]{:S(2)}) copy-start(pred[1024,512]{0,1:T(8,128)(4,1)} %copy-done.9) | copy-start | bytes 1572868
  865.9 18.0 %copy-start.16 = (f32[2,512,512]{1,2,0:T(8,128)S(1)}, f32[2,512,512]{1,2,0:T(8,128)}, u32[]{:S(2)}) copy-start(f32[2,512,512]{1,2,0:T(8,128)} %get-tuple-element.72) | copy-start | bytes 6291460
  898.0 22.9 %copy-start.1 = (f32[2,4]{1,0:T(2,128)S(1)}, f32[2,4]{1,0:T(2,128)}, u32[]{:S(2)}) copy-start(f32[2,4]{1,0:T(2,128)} %param.10) | copy-start | bytes 100
Sparse Core Ops, SparseCore 0:
  11.7 34.9 all-reduce.8
  52.6 62.5 all-reduce.10
  412.0 208.1 all-reduce.12
  747.2 118.6 all-reduce.14
Sparse Core Ops, SparseCore 1:
  54.5 24.2 all-gather.1
where the time goes:
time: 932 us; the launch traced here: 928 us
  waiting for transfers between devices  416 us (45%)
  other arithmetic  344 us (37%)
  matrix products  98.3 us (11%)
  local copies, waits for them, and re-layouts  53.7 us (6%)
  between operations  16.1 us (2%)
    psum x4, waiting for transfers between devices, spread(): return lax.psum(block, axis)  415 us
    another operation x16, other arithmetic, local(): factor = jnp.linalg.cholesky(diagonal)  158 us
    another operation x3, other arithmetic, local(): lax.linalg.triangular_solve(factor, block_sides, left_side=True, lower=True)  84.7 us
    another operation x3, other arithmetic, local(): lax.linalg.triangular_solve(factor, system_tiles, left_side=False, lower=...  78.9 us
    another operation x40, local copies, waits for them, and re-layouts  27.2 us
    dot_general x1, matrix products, local(): jnp.dot(panel[1], solved_sides, precision=lax.Precision.HIGHEST)  22.9 us
    another operation x7, matrix products, local(): lax.linalg.triangular_solve(factor, block_sides, left_side=True, lower=True)  20.6 us
  transfers between devices with their start and end apart: 5, of which 4 were waited for; matrix products, arithmetic and copies ran while one was open for 32% of the time, Pallas kernels for 0%

commit v1 on v0

--- a/solution.py
+++ b/solution.py
@@ -12,7 +12,7 @@
 
 def spread(block, axis, owner):
     block = jnp.where(lax.axis_index(axis) == owner, block, jnp.zeros_like(block))
-    return lax.psum(block, axis)
+    return jnp.sum(lax.all_gather(block, axis), axis=0)
 
 
 def local(

time: 932 us -> 1340 us (1.44)
  waiting for transfers between devices: 416 us -> 778 us
  other arithmetic: 344 us -> 393 us
    all_gather x0 -> x6, waiting for transfers between devices: none -> 777 us  [spread(): return jnp.sum(lax.all_gather(block, axis), axis=0)]
    psum x4 -> x0, waiting for transfers between devices: 415 us -> none  [spread(): return lax.psum(block, axis)]
    reduce_sum x0 -> x5, other arithmetic: none -> 43.9 us  [spread(): return jnp.sum(lax.all_gather(block, axis), axis=0)]
    another operation x16 -> x18, other arithmetic: 158 us -> 156 us  [local(): factor = jnp.linalg.cholesky(diagonal)]
    another operation x40 -> x24, local copies, waits for them, and re-layouts: 27.2 us -> 25.7 us
  transfers between devices with their start and end apart: 5 -> 7, of which waited for: 4 -> 6; matrix products, arithmetic and copies ran while one was open for 32% -> 38% of each run, Pallas kernels for 0% -> 0%
where the time goes in v1:
time: 1340 us
  waiting for transfers between devices  778 us (58%)
  other arithmetic  393 us (29%)
  matrix products  104 us (8%)
  local copies, waits for them, and re-layouts  48.1 us (4%)
  between operations  14.9 us (1%)
    all_gather x6, waiting for transfers between devices, spread(): return jnp.sum(lax.all_gather(block, axis), axis=0)  777 us
    another operation x18, other arithmetic, local(): factor = jnp.linalg.cholesky(diagonal)  156 us
    another operation x3, other arithmetic, local(): lax.linalg.triangular_solve(factor, block_sides, left_side=True, lower=True)  85 us
    another operation x3, other arithmetic, local(): lax.linalg.triangular_solve(factor, system_tiles, left_side=False, lower=...  78.9 us
    reduce_sum x5, other arithmetic, spread(): return jnp.sum(lax.all_gather(block, axis), axis=0)  43.9 us
  transfers between devices with their start and end apart: 7, of which 6 were waited for; matrix products, arithmetic and copies ran while one was open for 38% of the time, Pallas kernels for 0%

profile of v1, /device:TPU:0, one launch (start us, length us, event | category | flops | bytes accessed | tf_op | source)
XLA Modules:
  0.0 1338.8 jit_solution(4512754469502060749)
XLA Ops:
  10.5 19.1 %all-gather.18.cloned.1.call-done = bf16[1024,512]{1,0:T(8,128)(2,1)} async-done(((bf16[256,512]{1,0:T(8,128)(2,1)}), bf16[1024,512]{1,0:T(8,128)(2,1)}) %all-gather.18.cloned.1.call-update) | async-done | bytes 1048592 | tf_op jit(solution)/shard_map/all_gather | solution.py:15
  41.2 56.2 %all-gather.20.cloned.1.call-done = f32[8,512,512]{2,1,0:T(8,128)} async-done(((f32[2,512,512]{2,1,0:T(8,128)}), f32[8,512,512]{2,1,0:T(8,128)}) %all-gather.20.cloned.1.call-update) | async-done | bytes 8388624 | tf_op jit(solution)/shard_map/all_gather | solution.py:15
  97.4 6.0 reduce_sum.60
  103.4 3.1 copy.114
  106.5 3.4 fusion.30
  111.3 23.5 %custom-call.37 = f32[2,128,128]{2,1,0:T(8,128)S(1)} custom-call(f32[2,128,128]{2,1,0:T(8,128)S(1)} %cholesky.271), custom_call_target="Cholesky" | custom-call | tf_op jit(solution)/shard_map/jit(cholesky)/cholesky | solution.py:63
  136.3 19.7 %custom-call.38 = f32[2,1,128,128]{2,3,1,0:T(8,128)S(1)} custom-call(f32[2,1,128,128]{3,2,1,0:T(8,128)S(1)} %select_bitcast_fusion.2), custom_call_target="InvertDiagBlocksLowerTriangular" | custom-call | tf_op jit(solution)/shard_map/jit(cholesky)/cholesky | solution.py:63
  159.8 23.5 %custom-call.39 = f32[2,128,128]{2,1,0:T(8,128)S(1)} custom-call(f32[2,128,128]{2,1,0:T(8,128)S(1)} %cholesky.275), custom_call_target="Cholesky" | custom-call | tf_op jit(solution)/shard_map/jit(cholesky)/cholesky | solution.py:63
  183.9 20.1 %custom-call.40 = f32[2,1,128,128]{2,3,1,0:T(8,128)S(1)} custom-call(f32[2,1,128,128]{3,2,1,0:T(8,128)S(1)} %get-tuple-element.83), custom_call_target="InvertDiagBlocksLowerTriangular" | custom-call | tf_op jit(solution)/shard_map/jit(cholesky)/cholesky | solution.py:63
  206.9 23.5 %custom-call.41 = f32[2,128,128]{2,1,0:T(8,128)S(1)} custom-call(f32[2,128,128]{2,1,0:T(8,128)S(1)} %cholesky.280), custom_call_target="Cholesky" | custom-call | tf_op jit(solution)/shard_map/jit(cholesky)/cholesky | solution.py:63
  231.0 19.7 %custom-call.42 = f32[2,1,128,128]{2,3,1,0:T(8,128)S(1)} custom-call(f32[2,1,128,128]{3,2,1,0:T(8,128)S(1)} %get-tuple-element.81), custom_call_target="InvertDiagBlocksLowerTriangular" | custom-call | tf_op jit(solution)/shard_map/jit(cholesky)/cholesky | solution.py:63
  253.4 23.5 %custom-call.43 = f32[2,128,128]{2,1,0:T(8,128)S(1)} custom-call(f32[2,128,128]{2,1,0:T(8,128)S(1)} %convolution_subtract_fusion.5), custom_call_target="Cholesky" | custom-call | tf_op jit(solution)/shard_map/jit(cholesky)/cholesky | solution.py:63
  278.1 4.3 fusion.31
  282.6 11.7 while.3
  289.0 2.3 bitcast_dynamic-update-slice_fusion.4
  294.2 78.8 %custom-call.44 = f32[2,4,128,128]{2,3,1,0:T(8,128)S(1)} custom-call(f32[2,4,128,128]{3,2,1,0:T(8,128)S(1)} %bitcast.123), custom_call_target="InvertDiagBlocksLowerTriangular" | custom-call | tf_op jit(solution)/shard_map/triangular_solve | solution.py:64
  373.0 2.4 fusion.39
  375.5 3.3 convolution_subtract_fusion.2
  379.8 4.5 fusion.33
  385.4 6.5 fusion.36
  393.0 3.0 fusion.7
  396.0 5.4 copy.129
  402.4 2.5 convolution_multiply_fusion
  405.0 3.4 copy-done.3
  410.1 99.2 %all-gather.24.cloned.1.call-done = f32[16,512,512]{2,1,0:T(8,128)} async-done(((f32[2,512,512]{2,1,0:T(8,128)}), f32[16,512,512]{2,1,0:T(8,128)}) %all-gather.24.cloned.1.call-update) | async-done | bytes 16777232 | tf_op jit(solution)/shard_map/all_gather | solution.py:15
  509.4 9.4 reduce_sum.64
  518.8 3.5 broadcast_select_fusion
  523.1 14.1 %while.4 = (s32[]{:T(128)}, f32[2,512,512]{2,1,0:T(8,128)}, s32[4,2]{0,1:T(2,128)S(1)}, f32[4,2,128,128]{3,2,0,1:T(8,128)}, s32[]{:T(128)}) while((s32[]{:T(128)}, f32[2,512,512]{2,1,0:T(8,128)}, s32[4,2]{0,1:T(2,128)S(1)}, f32[4,2,128,128]{3,2,0,1:T(8,128)}, s32[]{:T(128)}) %tuple.79), condition=%wide.while_cond.2, body=%wide.while_body.2.sunk | while | flops 2 | bytes 263277 | solution.py:77
  523.7 2.9 bitcast_dynamic-update-slice_fusion.5
  527.3 2.9 bitcast_dynamic-update-slice_fusion.5
  530.8 2.9 bitcast_dynamic-update-slice_fusion.5
  534.3 2.9 bitcast_dynamic-update-slice_fusion.5
  537.2 80.5 %custom-call.45 = f32[2,4,128,128]{2,3,1,0:T(8,128)} custom-call(f32[2,4,128,128]{3,2,1,0:T(8,128)} %bitcast.124), custom_call_target="InvertDiagBlocksLowerTriangular" | custom-call | tf_op jit(solution)/shard_map/triangular_solve | solution.py:77
  617.7 3.3 fusion.41
  621.0 3.0 convolution_subtract_fusion
  625.9 3.3 fusion.18
  631.2 5.2 fusion.21
  639.5 3.3 fusion.6
  642.8 503.9 %all-gather.12.cloned.1.call-done = f32[8,2,1024,512]{3,2,1,0:T(8,128)} async-done(((f32[1,2,1024,512]{3,2,1,0:T(8,128)}), f32[8,2,1024,512]{3,2,1,0:T(8,128)}) %all-gather.12.cloned.1.call-update) | async-done | bytes 33554448 | tf_op jit(solution)/shard_map/all_gather | solution.py:15
  1146.7 16.8 %reduce_sum.62 = f32[2,1024,512]{2,1,0:T(8,128)} reduce(f32[8,2,1024,512]{3,2,1,0:T(8,128)} %all-gather.12.cloned.1.call-done, f32[]{:T(128)} %constant.237.clone.1), dimensions={0}, to_apply=%region_10.11 | reduce | flops 7340032 | bytes 37748740 | tf_op jit(solution)/shard_map/reduce_sum | solution.py:15
  1163.6 3.8 dynamic-slice_select_fusion
  1167.4 87.2 %all-gather.16.cloned.1.call-done = f32[4,512,2048]{2,1,0:T(8,128)} async-done(((f32[1,512,2048]{2,1,0:T(8,128)}), f32[4,512,2048]{2,1,0:T(8,128)}) %all-gather.16.cloned.1.call-update) | async-done | bytes 16777232 | tf_op jit(solution)/shard_map/all_gather | solution.py:15
  1254.6 10.3 reduce_sum.65
  1264.9 17.6 %fusion.24 = f32[1024,2048]{1,0:T(8,128)S(1)} fusion(f32[512,2048]{1,0:T(8,128)} %reduce_sum.65, f32[2,1024,512]{2,1,0:T(8,128)} %reduce_sum.62), kind=kOutput, calls=%fused_computation.34 | convolution fusion | flops 12884901888 | bytes 14680064 | tf_op jit(solution)/shard_map/dot_general | solution.py:83
  1282.4 20.4 %subtract_select_fusion = f32[1024,2048]{1,0:T(8,128)} fusion(f32[1024,2048]{1,0:T(8,128)} %copy-done.3, f32[1024,2048]{1,0:T(8,128)S(1)} %fusion.24, f32[512,2048]{1,0:T(8,128)} %reduce_sum.65, pred[1024]{0:T(1024)(128)(4,1)S(1)} %compare_and_fusion, pred[2048]{0:T(1024)(128)(4,1)S(1)} %eq.76, f32[2,1024,512]{2,1,0:T(8,128)S(1)} %copy-done.2), kind=kOutput, calls=%fused_computation.5 | convolution fusion | flops 12891193344 | bytes 35654656 | tf_op jit(solution)/shard_map/dot_general | solution.py:84
  1302.9 11.6 all-gather.22.cloned.1.call-done
  1314.5 6.0 reduce_sum.63
  1320.5 11.2 convolution_subtract_fusion.1
  (113 shorter events, 55.3 us)
Async XLA Ops:
  7.2 2.0 copy-start
  7.2 23.9 %copy-start.11 = (bf16[256,1024]{1,0:T(8,128)(2,1)S(1)}, bf16[256,1024]{1,0:T(8,128)(2,1)}, u32[]{:S(2)}) copy-start(bf16[256,1024]{1,0:T(8,128)(2,1)} %param.7) | copy-start | bytes 1572868
  7.2 22.4 %all-gather.18.cloned.1.call-start = ((), (), s32[]{:S(2)}) async-start(), calls=%async_computation.3 | async-start | bytes 1310720 | tf_op jit(solution)/shard_map/all_gather | solution.py:15
  9.0 88.4 %all-gather.20.cloned.1.call-start = ((), (), s32[]{:S(2)}) async-start(), calls=%async_computation.4 | async-start | bytes 10485760 | tf_op jit(solution)/shard_map/all_gather | solution.py:15
  10.5 24.3 %copy-start.7 = (pred[1024,512]{1,0:T(8,128)(4,1)}, pred[1024,512]{1,0:T(8,128)(4,1)S(1)}, u32[]{:S(2)}) copy-start(pred[1024,512]{1,0:T(8,128)(4,1)S(1)} %broadcast_compare_fusion) | copy-start | bytes 1572868
  35.4 2.0 copy-start.4
  39.0 363.2 %all-gather.14.cloned.1.call-start = ((), (), s32[]{:S(2)}) async-start(), calls=%async_computation.1 | async-start | bytes 1572864 | tf_op jit(solution)/shard_map/all_gather | solution.py:50
  39.8 469.6 %all-gather.24.cloned.1.call-start = ((), (), s32[]{:S(2)}) async-start(), calls=%async_computation.6 | async-start | bytes 18874368 | tf_op jit(solution)/shard_map/all_gather | solution.py:15
  109.9 1.3 copy-start.6
  282.4 864.3 %all-gather.12.cloned.1.call-start = ((), (), s32[]{:S(2)}) async-start(), calls=%async_computation | async-start | bytes 37748736 | tf_op jit(solution)/shard_map/all_gather | solution.py:15
  375.5 4.4 copy-start.5
  401.4 0.7 copy-start.14
  401.4 1.1 copy-start.12
  401.4 853.2 %all-gather.16.cloned.1.call-start = ((), (), s32[]{:S(2)}) async-start(), calls=%async_computation.2 | async-start | bytes 20971520 | tf_op jit(solution)/shard_map/all_gather | solution.py:15
  405.0 3.4 copy-start.3
  617.7 3.3 copy-start.9
  621.0 3.0 copy-start.13
  624.0 2.0 copy-start.10
  642.7 671.7 %all-gather.22.cloned.1.call-start = ((), (), s32[]{:S(2)}) async-start(), calls=%async_computation.5 | async-start | bytes 10485760 | tf_op jit(solution)/shard_map/all_gather | solution.py:15
  1264.9 17.6 %copy-start.2 = (f32[2,1024,512]{2,1,0:T(8,128)S(1)}, f32[2,1024,512]{2,1,0:T(8,128)}, u32[]{:S(2)}) copy-start(f32[2,1024,512]{2,1,0:T(8,128)} %reduce_sum.62) | copy-start | bytes 12582916
  1314.5 6.0 copy-start.8
  1320.5 11.2 copy-start.1
Sparse Core Ops, SparseCore 0:
  10.1 19.4 all-gather.17
  39.1 58.2 all-gather.19
  99.0 21.2 all-gather.13
  282.5 226.7 all-gather.23
  510.7 635.9 all-gather.11
  1148.7 105.8 all-gather.15
  1256.2 58.2 all-gather.21
